TPU v7x, 32 devices: a whole 2x2x4 slice. The times are simulated.
32 devices in a mesh: seq: 8 (over y, x, core), sub: 4 (over z).
Axes of the slice: x: 2, y: 2, z: 4, core: 2. Of those that a mesh axis runs over, the one named last changes fastest.
Arguments:
- query_rows: bfloat16 [8192, 1120], P(('seq', 'sub')), may hold values from -6 to 6
- key_rows: bfloat16 [8192, 1120], P(('seq', 'sub')), may hold values from -6 to 6
- value_rows: bfloat16 [8192, 1120], P(('seq', 'sub')), may hold values from -6 to 6
- query_tangent: bfloat16 [8192, 1120], P(('seq', 'sub')), may hold values from -6 to 6
- key_tangent: bfloat16 [8192, 1120], P(('seq', 'sub')), may hold values from -6 to 6
- value_tangent: bfloat16 [8192, 1120], P(('seq', 'sub')), may hold values from -6 to 6
- teacher: bfloat16 [8192, 2240], P(('seq', 'sub')), may hold values from -64 to 64
- out_weight: bfloat16 [1120, 2240], replicated, may hold values from -0.1875 to 0.1875
- norm_gain: float32 [1120], replicated, may hold values from 0.1 to 1.9
- clip_length: int32 [1], replicated, may hold values from 4096 to 8192
- block_mask: int32 [128], P(('seq', 'sub')), may hold values 0 or 1
Outputs:
- residual: bfloat16 [8192, 2240], P(('seq', 'sub'))
- grad_query: bfloat16 [8192, 1120], P(('seq', 'sub'))
- grad_key: bfloat16 [8192, 1120], P(('seq', 'sub'))
- grad_value: bfloat16 [8192, 1120], P(('seq', 'sub'))
All inputs are finite; a program needn't handle non-finite values. No bound on the sum of `block_mask` on one device may be relied on, other than what follows from the above.
Results may differ from a plain program's by a relative error of at most 0.007.
Values may be sent and summed in bfloat16 or wider, within the bound.
A program may use at most 64 MiB of HBM per device.

v0:
```python
import jax
import jax.numpy as jnp
from jax import lax
from jax.sharding import PartitionSpec as P

H = 10
E = 112
BLK = 64


def split_heads(matrix):
    return matrix.reshape(matrix.shape[0], H, E)


def norm_back(unnorm, scale_inv, weighted):
    inner_mean = jnp.mean(unnorm * weighted, axis=-1, keepdims=True)
    return scale_inv * weighted - unnorm * (scale_inv * scale_inv * scale_inv) * inner_mean


def combine_states(stacked):
    totals = lax.psum(stacked, ("seq", "sub"))
    return totals.astype(jnp.bfloat16)


def local(
    query_rows,
    key_rows,
    value_rows,
    query_tangent,
    key_tangent,
    value_tangent,
    teacher,
    out_weight,
    norm_gain,
    clip_length,
    block_mask,
):
    f32 = jnp.float32
    bf16 = jnp.bfloat16
    tok_rows = query_rows.shape[0]
    first_row = (lax.axis_index("seq") * lax.axis_size("sub") + lax.axis_index("sub")) * tok_rows
    position = first_row + lax.iota(jnp.int32, tok_rows)
    block_flags = jnp.broadcast_to(block_mask[:, None], (tok_rows // BLK, BLK)).reshape(tok_rows)
    valid_rows = jnp.where((position < clip_length[0]) & (block_flags == 1), 1.0, 0.0).astype(f32)[
        :, None
    ]
    key_vals = key_rows.astype(f32)
    key_feat = (valid_rows * jnp.maximum(key_vals, 0.0)).astype(bf16)
    key_slope = valid_rows * jnp.where(key_vals > 0, 1.0, 0.0).astype(f32)
    key_dot = (key_slope * key_tangent.astype(f32)).astype(bf16)
    value_heads = split_heads(value_rows)
    feat_keys = split_heads(key_feat)
    state_part = jnp.einsum("the,thf->hef", feat_keys, value_heads, preferred_element_type=f32)
    tangent_part = jnp.einsum(
        "the,thf->hef", split_heads(key_dot), value_heads, preferred_element_type=f32
    ) + jnp.einsum(
        "the,thf->hef", feat_keys, split_heads(value_tangent), preferred_element_type=f32
    )
    states = combine_states(jnp.stack([state_part, tangent_part]))
    state = states[0]
    state_dot = states[1]
    query_vals = query_rows.astype(f32)
    query_feat = jnp.maximum(query_vals, 0.0).astype(bf16)
    query_slope = jnp.where(query_vals > 0, 1.0, 0.0).astype(f32)
    query_dot = (query_slope * query_tangent.astype(f32)).astype(bf16)
    feat_heads = split_heads(query_feat)
    unnorm = jnp.einsum("the,hef->thf", feat_heads, state, preferred_element_type=f32)
    unnorm_dot = jnp.einsum(
        "the,hef->thf", split_heads(query_dot), state, preferred_element_type=f32
    ) + jnp.einsum("the,hef->thf", feat_heads, state_dot, preferred_element_type=f32)
    gain_heads = norm_gain.reshape(H, E)
    scale_inv = lax.rsqrt(jnp.mean(unnorm * unnorm, axis=-1, keepdims=True) + 1e-06)
    normed_dot = (
        (gain_heads * norm_back(unnorm, scale_inv, unnorm_dot))
        .astype(bf16)
        .reshape(tok_rows, H * E)
    )
    velocity = jnp.dot(normed_dot, out_weight, preferred_element_type=f32)
    residual = (velocity - teacher.astype(f32)).astype(bf16)
    normed_grad = lax.dot_general(
        residual, out_weight, (((1,), (1,)), ((), ())), preferred_element_type=f32
    )
    unnorm_grad = norm_back(unnorm, scale_inv, gain_heads * split_heads(normed_grad)).astype(bf16)
    grad_part = jnp.einsum("the,thf->hef", feat_heads, unnorm_grad, preferred_element_type=f32)
    state_grad = combine_states(grad_part[None])[0]
    grad_query = (
        query_slope
        * jnp.einsum("thf,hef->the", unnorm_grad, state, preferred_element_type=f32).reshape(
            tok_rows, H * E
        )
    ).astype(bf16)
    grad_key = (
        key_slope
        * jnp.einsum("thf,hef->the", value_heads, state_grad, preferred_element_type=f32).reshape(
            tok_rows, H * E
        )
    ).astype(bf16)
    grad_value = (
        jnp.einsum("the,hef->thf", feat_keys, state_grad, preferred_element_type=f32)
        .reshape(tok_rows, H * E)
        .astype(bf16)
    )
    return (residual, grad_query, grad_key, grad_value)


def solution(mesh):
    return jax.shard_map(
        local,
        mesh=mesh,
        in_specs=(
            P(("seq", "sub"), None),
            P(("seq", "sub"), None),
            P(("seq", "sub"), None),
            P(("seq", "sub"), None),
            P(("seq", "sub"), None),
            P(("seq", "sub"), None),
            P(("seq", "sub"), None),
            P(),
            P(),
            P(),
            P(("seq", "sub")),
        ),
        out_specs=(
            P(("seq", "sub"), None),
            P(("seq", "sub"), None),
            P(("seq", "sub"), None),
            P(("seq", "sub"), None),
        ),
        check_vma=False,
    )
```

profile of v0, /device:TPU:0, one launch (start us, length us, event | category | flops | bytes accessed | tf_op | source)
XLA Modules:
  0.0 119.9 jit_solution(6810560053801250112)
XLA Ops:
  0.6 0.0 copy-start
  1.4 0.4 copy-done
  1.7 0.7 broadcast_compare_fusion
  2.4 0.1 broadcast_in_dim.29
  2.4 0.1 eq.16
  2.5 0.8 mul.117
  3.3 1.6 %fusion.4 = (bf16[256,1120]{0,1:T(8,128)(2,1)S(1)}, bf16[256,1120]{0,1:T(8,128)(2,1)S(1)}) fusion(bf16[256,1120]{0,1:T(8,128)(2,1)} %param.12, f32[256]{0:T(256)S(1)} %and_select_fusion, bf16[256,1120]{0,1:T(8,128)(2,1)} %param.15), kind=kLoop, calls=%fused_computation.17 | loop fusion | flops 2867200 | bytes 2294784 | tf_op jit(solution)/shard_map/convert_element_type | solution.py:48
  4.9 0.0 copy-start.3
  5.0 0.3 fusion.16
  5.3 0.7 copy-done.3
  6.0 0.3 fusion.2
  6.3 0.3 convolution_bitcast_fusion.2
  6.6 0.1 pad_maximum_fusion
  6.7 0.0 copy-start.1
  6.7 53.7 %all-reduce.2 = bf16[2,10,112,112]{3,2,1,0:T(8,128)(2,1)S(1)} all-reduce(f32[2,10,112,112]{3,2,1,0:T(8,128)S(1)} %pad_maximum_fusion), channel_id=1, replica_groups=mesh['seq'=8,'sub'=4] {'seq','sub'}, use_global_device_ids=true, to_apply=%region_0.1 | all-reduce | flops 250880 | bytes 1505280 | tf_op jit(solution)/shard_map/psum | solution.py:21
  60.4 0.0 copy-done.1
  60.5 0.0 slice-start
  60.5 1.5 %fusion.5 = (bf16[256,1120]{0,1:T(8,128)(2,1)S(1)}, bf16[256,1120]{0,1:T(8,128)(2,1)S(1)}) fusion(bf16[256,1120]{0,1:T(8,128)(2,1)S(1)} %copy-done.1, bf16[256,1120]{0,1:T(8,128)(2,1)} %param.14), kind=kLoop, calls=%fused_computation.18 | loop fusion | flops 2293760 | bytes 2293760 | tf_op jit(solution)/shard_map/convert_element_type | solution.py:63
  61.9 0.4 fusion.13
  62.3 0.0 slice-start.1
  62.3 0.4 fusion.1
  62.7 0.4 multiply_reduce_fusion.2
  63.1 0.0 copy-start.4
  63.1 0.6 multiply_convert_fusion
  63.7 0.0 slice-done
  63.7 0.0 slice-done.1
  63.7 0.7 copy-done.4
  64.5 2.3 %fusion = bf16[256,2240]{0,1:T(8,128)(2,1)S(1)} fusion(bf16[256,1120]{0,1:T(8,128)(2,1)S(1)} %bitcast.81, bf16[1120,2240]{1,0:T(8,128)(2,1)S(1)} %bitcast.83, bf16[256,2240]{0,1:T(8,128)(2,1)S(1)} %copy-done.4), kind=kOutput, calls=%fused_computation.1 | convolution fusion | flops 1286225920 | bytes 7884800 | tf_op jit(solution)/shard_map/dot_general | solution.py:78
  66.8 0.0 copy-start.5
  66.8 1.5 %fusion.17 = f32[256,1120]{0,1:T(8,128)S(1)} fusion(bf16[1120,2240]{1,0:T(8,128)(2,1)S(1)} %bitcast.83, bf16[256,2240]{0,1:T(8,128)(2,1)S(1)} %fusion), kind=kOutput, calls=%fused_computation.47 | convolution fusion | flops 1284505600 | bytes 7311360 | tf_op jit(solution)/shard_map/dot_general | solution.py:80
  68.3 0.0 copy-done.5
  68.3 0.2 multiply_reduce_fusion
  68.6 0.3 subtract_convert_fusion
  68.9 0.3 convolution_bitcast_fusion.1
  69.2 0.3 fusion.12
  69.5 1.0 fusion.7
  70.5 46.1 %all-reduce.3 = bf16[1,10,112,112]{3,2,1,0:T(8,128)(2,1)S(1)} all-reduce(f32[1,10,112,112]{3,2,1,0:T(8,128)S(1)} %convolution_bitcast_fusion.1), channel_id=1, replica_groups=mesh['seq'=8,'sub'=4] {'seq','sub'}, use_global_device_ids=true, to_apply=%region_4.5 | all-reduce | flops 125440 | bytes 752640 | tf_op jit(solution)/shard_map/psum | solution.py:21
  116.6 1.2 convolution_convert_fusion
  117.8 0.0 copy-start.2
  117.8 0.3 fusion.10
  118.1 0.8 copy-done.2
  118.9 1.0 fusion.8
  (4 shorter events, 0.0 us)
Async XLA Ops:
  0.6 1.1 copy-start
  4.9 1.1 copy-start.3
  6.7 53.7 %copy-start.1 = (bf16[256,1120]{0,1:T(8,128)(2,1)S(1)}, bf16[256,1120]{0,1:T(8,128)(2,1)}, u32[]{:S(2)}) copy-start(bf16[256,1120]{0,1:T(8,128)(2,1)} %param.11) | copy-start | bytes 1720324
  60.5 3.3 %slice-start = ((s8[5160960]{0:T(1024)(128)(4,1)}), s8[4194304]{0:T(1024)(128)(4,1)S(1)}, s32[]{:S(2)}) async-start(s8[5160960]{0:T(1024)(128)(4,1)} %bitcast.82), calls=%async_computation | async-start | bytes 8388608
  62.3 1.4 %slice-start.1 = ((s8[5160960]{0:T(1024)(128)(4,1)}), s8[966656]{0:T(1024)(128)(4,1)S(1)}, s32[]{:S(2)}) async-start(s8[5160960]{0:T(1024)(128)(4,1)} %bitcast.82), calls=%async_computation.1 | async-start | bytes 1933312
  63.1 1.3 %copy-start.4 = (bf16[256,2240]{0,1:T(8,128)(2,1)S(1)}, bf16[256,2240]{0,1:T(8,128)(2,1)}, u32[]{:S(2)}) copy-start(bf16[256,2240]{0,1:T(8,128)(2,1)} %param.17) | copy-start | bytes 3440644
  66.8 1.5 %copy-start.5 = (bf16[256,2240]{0,1:T(8,128)(2,1)}, bf16[256,2240]{0,1:T(8,128)(2,1)S(1)}, u32[]{:S(2)}) copy-start(bf16[256,2240]{0,1:T(8,128)(2,1)S(1)} %fusion) | copy-start | bytes 3440644
  117.8 1.1 copy-start.2
where the time goes:
time: 120 us
  blocking collectives  99.8 us (83%)
  matrix products  7.92 us (7%)
  other arithmetic  7.01 us (6%)
  local copies, waits for them, and re-layouts  3.56 us (3%)
  between operations  1.56 us (1%)
    psum x2, blocking collectives, combine_states(): totals = lax.psum(stacked, ('seq', 'sub'))  99.8 us
    unnamed x16, local copies, waits for them, and re-layouts  2.62 us

commit v1 on v0

--- a/solution.py
+++ b/solution.py
@@ -1,6 +1,10 @@
+import functools
+
 import jax
 import jax.numpy as jnp
 from jax import lax
+from jax.experimental import pallas as pl
+from jax.experimental.pallas import tpu as pltpu
 from jax.sharding import PartitionSpec as P
 
 H = 10
@@ -17,9 +21,170 @@
     return scale_inv * weighted - unnorm * (scale_inv * scale_inv * scale_inv) * inner_mean
 
 
-def combine_states(stacked):
-    totals = lax.psum(stacked, ("seq", "sub"))
-    return totals.astype(jnp.bfloat16)
+MESH = pl.DeviceIdType.MESH
+
+
+def total_kernel(
+    outer, x_ref, out_ref, half, mine, parts, s0, r0, s1, r1, s2, r2, s3, r3
+):
+    seq = lax.axis_index("seq")
+    sub = lax.axis_index("sub")
+    depth = lax.axis_size("sub")
+    chips = outer
+    core = lax.rem(seq, 2)
+    chip = (seq // 2) * depth + sub
+    partner = (seq + 1 - 2 * core, sub)
+
+    def peer(index):
+        return (index // depth) * 2 + core, lax.rem(index, depth)
+
+    def ahead(step):
+        return lax.rem(chip + step, chips)
+
+    def behind(step):
+        return lax.rem(chip + chips - step, chips)
+
+    barrier = pltpu.get_barrier_semaphore()
+    pl.semaphore_signal(barrier, inc=1, device_id=partner, device_id_type=MESH)
+
+    @pl.loop(1, chips)
+    def _(step):
+        pl.semaphore_signal(barrier, inc=1, device_id=peer(ahead(step)), device_id_type=MESH)
+
+    pl.semaphore_wait(barrier, chips)
+
+    swap = pltpu.make_async_remote_copy(
+        src_ref=x_ref.at[1 - core],
+        dst_ref=half,
+        send_sem=s0,
+        recv_sem=r0,
+        device_id=partner,
+        device_id_type=MESH,
+    )
+    swap.start()
+    swap.wait()
+
+    def scatter(index):
+        return pltpu.make_async_remote_copy(
+            src_ref=mine.at[index],
+            dst_ref=parts.at[chip],
+            send_sem=s1.at[index],
+            recv_sem=r1.at[chip],
+            device_id=peer(index),
+            device_id_type=MESH,
+        )
+
+    def scattered(index):
+        return pltpu.make_async_remote_copy(
+            src_ref=mine.at[index],
+            dst_ref=parts.at[index],
+            send_sem=s1.at[index],
+            recv_sem=r1.at[index],
+            device_id=peer(index),
+            device_id_type=MESH,
+        )
+
+    def pair(index):
+        return x_ref[core, index].astype(jnp.float32) + half[index].astype(jnp.float32)
+
+    @pl.loop(1, chips)
+    def _(step):
+        index = ahead(step)
+        mine[index] = pair(index).astype(mine.dtype)
+        scatter(index).start()
+
+    def add(step, acc):
+        index = behind(step)
+        scattered(index).wait_recv()
+        return acc + parts[index].astype(jnp.float32)
+
+    total = lax.fori_loop(1, chips, add, pair(chip))
+    out_ref[core, chip] = total.astype(out_ref.dtype)
+
+    def gather(index):
+        return pltpu.make_async_remote_copy(
+            src_ref=out_ref.at[core, chip],
+            dst_ref=out_ref.at[core, chip],
+            send_sem=s2.at[index],
+            recv_sem=r2.at[chip],
+            device_id=peer(index),
+            device_id_type=MESH,
+        )
+
+    def gathered(index):
+        return pltpu.make_async_remote_copy(
+            src_ref=out_ref.at[core, chip],
+            dst_ref=out_ref.at[core, index],
+            send_sem=s2.at[index],
+            recv_sem=r2.at[index],
+            device_id=peer(index),
+            device_id_type=MESH,
+        )
+
+    def forward(index):
+        return pltpu.make_async_remote_copy(
+            src_ref=out_ref.at[core, index],
+            dst_ref=out_ref.at[core, index],
+            send_sem=s3.at[index],
+            recv_sem=r3.at[index],
+            device_id=partner,
+            device_id_type=MESH,
+        )
+
+    def forwarded(index):
+        return pltpu.make_async_remote_copy(
+            src_ref=out_ref.at[core, index],
+            dst_ref=out_ref.at[1 - core, index],
+            send_sem=s3.at[index],
+            recv_sem=r3.at[index],
+            device_id=partner,
+            device_id_type=MESH,
+        )
+
+    @pl.loop(1, chips)
+    def _(step):
+        gather(ahead(step)).start()
+
+    forward(chip).start()
+
+    @pl.loop(1, chips)
+    def _(step):
+        index = behind(step)
+        gathered(index).wait_recv()
+        forward(index).start()
+
+    @pl.loop(1, chips)
+    def _(step):
+        index = ahead(step)
+        scatter(index).wait_send()
+        gather(index).wait_send()
+
+    @pl.loop(0, chips)
+    def _(step):
+        index = behind(step)
+        forwarded(index).wait_recv()
+        forward(index).wait_send()
+
+
+def combine_states(stacked, collective_id):
+    mats, rows, cols = stacked.shape
+    chips = lax.axis_size("seq") // 2 * lax.axis_size("sub")
+    piece = -(-(mats * rows) // (32 * chips)) * 16
+    flat = stacked.reshape(mats * rows, cols).astype(jnp.bfloat16)
+    flat = jnp.pad(flat, ((0, 2 * chips * piece - mats * rows), (0, 0)))
+    grid = flat.reshape(2, chips, piece, cols)
+    dma = pltpu.SemaphoreType.DMA
+    totals = pl.pallas_call(
+        functools.partial(total_kernel, chips),
+        out_shape=jax.ShapeDtypeStruct(grid.shape, jnp.bfloat16),
+        in_specs=[pl.BlockSpec(memory_space=pltpu.VMEM)],
+        out_specs=pl.BlockSpec(memory_space=pltpu.VMEM),
+        scratch_shapes=[pltpu.VMEM(grid.shape[1:], jnp.bfloat16)] * 3
+        + [dma, dma]
+        + [dma((chips,))] * 6,
+        compiler_params=pltpu.CompilerParams(collective_id=collective_id, has_side_effects=True),
+    )(grid)
+    return totals.reshape(2 * chips * piece, cols)[: mats * rows].reshape(mats, rows, cols)
 
 
 def local(
@@ -56,9 +221,9 @@
     ) + jnp.einsum(
         "the,thf->hef", feat_keys, split_heads(value_tangent), preferred_element_type=f32
     )
-    states = combine_states(jnp.stack([state_part, tangent_part]))
-    state = states[0]
-    state_dot = states[1]
+    states = combine_states(jnp.concatenate([state_part, tangent_part]), 0)
+    state = states[:H]
+    state_dot = states[H:]
     query_vals = query_rows.astype(f32)
     query_feat = jnp.maximum(query_vals, 0.0).astype(bf16)
     query_slope = jnp.where(query_vals > 0, 1.0, 0.0).astype(f32)
@@ -82,7 +247,7 @@
     )
     unnorm_grad = norm_back(unnorm, scale_inv, gain_heads * split_heads(normed_grad)).astype(bf16)
     grad_part = jnp.einsum("the,thf->hef", feat_heads, unnorm_grad, preferred_element_type=f32)
-    state_grad = combine_states(grad_part[None])[0]
+    state_grad = combine_states(grad_part, 1)
     grad_query = (
         query_slope
         * jnp.einsum("thf,hef->the", unnorm_grad, state, preferred_element_type=f32).reshape(

time: 120 us -> 73.7 us (0.61)
  blocking collectives: 99.8 us -> 0 us
  Pallas kernels: 0 us -> 50.2 us
  local copies, waits for them, and re-layouts: 3.56 us -> 7.58 us
    psum x2 -> x0, blocking collectives: 99.8 us -> none  [combine_states(): totals = lax.psum(stacked, ('seq', 'sub'))]
    pallas_call x0 -> x2, Pallas kernels: none -> 50.2 us  [combine_states(): pl.pallas_call(functools.partial(total_kernel, chips), out_shape=jax.Shap...]
    slice x0 -> x2, local copies, waits for them, and re-layouts: none -> 2.06 us  [the longest x1 1.08 us: local(): state_dot = states[H:]]
    pad x0 -> x2, local copies, waits for them, and re-layouts: none -> 1.78 us  [combine_states(): flat = jnp.pad(flat, ((0, 2 * chips * piece - mats * rows), (0, 0)))]
    unnamed x16 -> x18, local copies, waits for them, and re-layouts: 2.62 us -> 2.8 us
where the time goes in v1:
time: 73.7 us; the launch traced here: 73.2 us
  Pallas kernels  50.2 us (68%)
  matrix products  7.92 us (11%)
  local copies, waits for them, and re-layouts  7.58 us (10%)
  other arithmetic  5.95 us (8%)
  between operations  1.56 us (2%)
    pallas_call x2, Pallas kernels, combine_states(): pl.pallas_call(functools.partial(total_kernel, chips), out_shape=jax.Shap...  50.2 us
    unnamed x18, local copies, waits for them, and re-layouts  2.8 us
    dot_general x1, matrix products, local(): velocity = jnp.dot(normed_dot, out_weight, preferred_element_type=f32)  2.33 us
    pad x2, local copies, waits for them, and re-layouts, combine_states(): flat = jnp.pad(flat, ((0, 2 * chips * piece - mats * rows), (0, 0)))  1.78 us
    convert_element_type x1, other arithmetic, local(): key_feat = (valid_rows * jnp.maximum(key_vals, 0.0)).astype(bf16)  1.63 us
    dot_general x1, matrix products, local(): lax.dot_general(residual, out_weight, (((1,), (1,)), ((), ())), preferred...  1.51 us

profile of v1, /device:TPU:0, one launch (start us, length us, event | category | flops | bytes accessed | tf_op | source)
XLA Modules:
  0.0 73.2 jit_solution(17302860433538211914)
XLA Ops:
  0.6 0.0 copy-start
  1.4 0.4 copy-done
  1.7 0.7 broadcast_compare_fusion
  2.4 0.1 broadcast_in_dim.26
  2.4 0.1 eq.16
  2.5 0.8 %mul.117 = f32[10,112]{1,0:T(8,128)S(1)} reshape(f32[1120]{0:T(1024)} %param.19) | data formatting | bytes 8960 | tf_op jit(solution)/shard_map/mul | solution.py:239
  3.3 1.6 %fusion.4 = (bf16[256,1120]{0,1:T(8,128)(2,1)S(1)}, bf16[256,1120]{0,1:T(8,128)(2,1)S(1)}) fusion(bf16[256,1120]{0,1:T(8,128)(2,1)} %param.12, f32[256]{0:T(256)S(1)} %and_select_fusion, bf16[256,1120]{0,1:T(8,128)(2,1)} %param.15), kind=kLoop, calls=%fused_computation.17 | loop fusion | flops 2867200 | bytes 2294784 | tf_op jit(solution)/shard_map/convert_element_type | solution.py:213
  4.9 0.0 copy-start.4
  5.0 0.3 fusion.10
  5.3 0.8 %copy-done.4 = bf16[256,1120]{0,1:T(8,128)(2,1)S(1)} copy-done((bf16[256,1120]{0,1:T(8,128)(2,1)S(1)}, bf16[256,1120]{0,1:T(8,128)(2,1)}, u32[]{:S(2)}) %copy-start.4) | copy-done | bytes 573464
  6.0 0.3 fusion.2
  6.3 0.3 convolution_convert_fusion.2
  6.6 0.1 pad_maximum_fusion
  6.8 1.0 %pad.8 = bf16[2560,112]{1,0:T(8,128)(2,1)} pad(bf16[2240,112]{1,0:T(8,128)(2,1)S(1)} %bitcast.78, bf16[]{:T(256)} %constant.27.clone.1), padding=0_320x0_0 | pad | bytes 1075202 | tf_op jit(solution)/shard_map/jit(_pad)/pad | solution.py:174
  7.7 0.0 copy-start.1
  7.7 0.0 copy-start.3
  7.7 29.6 %shard_map.138 = bf16[2,16,80,112]{3,2,1,0:T(8,128)(2,1)} custom-call(bf16[2,16,80,112]{3,2,1,0:T(8,128)(2,1)} %bitcast.74), custom_call_target="tpu_custom_call" | custom-call | tf_op jit(solution)/shard_map/pallas_call | solution.py:177
  37.3 1.1 %fusion.9 = (bf16[1120,112]{1,0:T(8,128)(2,1)S(1)}, bf16[1120,112]{1,0:T(8,128)(2,1)S(1)}) fusion(bf16[2560,112]{1,0:T(8,128)(2,1)} %bitcast.77), kind=kLoop, calls=%fused_computation.37 | loop fusion | bytes 1003520 | tf_op jit(solution)/shard_map/slice | solution.py:226
  38.4 0.0 copy-done.1
  38.4 0.0 copy-done.3
  38.4 0.0 slice-start
  38.5 0.3 fusion.5
  38.8 0.4 fusion.11
  39.1 0.0 slice-start.1
  39.2 0.4 fusion.1
  39.5 0.4 multiply_reduce_fusion.2
  40.0 0.0 copy-start.5
  40.0 0.6 multiply_convert_fusion
  40.6 0.1 slice-done
  40.6 0.4 slice-done.1
  41.1 0.4 copy-done.5
  41.4 2.3 %fusion = bf16[256,2240]{0,1:T(8,128)(2,1)S(1)} fusion(bf16[256,1120]{0,1:T(8,128)(2,1)S(1)} %bitcast.87, bf16[1120,2240]{1,0:T(8,128)(2,1)S(1)} %bitcast.89, bf16[256,2240]{0,1:T(8,128)(2,1)S(1)} %copy-done.5), kind=kOutput, calls=%fused_computation.1 | convolution fusion | flops 1286225920 | bytes 7884800 | tf_op jit(solution)/shard_map/dot_general | solution.py:243
  43.8 0.0 copy-start.6
  43.8 1.5 %fusion.14 = f32[256,1120]{0,1:T(8,128)S(1)} fusion(bf16[1120,2240]{1,0:T(8,128)(2,1)S(1)} %bitcast.89, bf16[256,2240]{0,1:T(8,128)(2,1)S(1)} %fusion), kind=kOutput, calls=%fused_computation.42 | convolution fusion | flops 1284505600 | bytes 7311360 | tf_op jit(solution)/shard_map/dot_general | solution.py:245
  45.3 0.0 copy-done.6
  45.3 0.2 multiply_reduce_fusion
  45.6 0.3 subtract_convert_fusion
  45.9 0.3 convolution_convert_fusion.1
  46.2 0.8 %pad.9 = bf16[1536,112]{1,0:T(8,128)(2,1)} pad(bf16[1120,112]{1,0:T(8,128)(2,1)S(1)} %bitcast.84, bf16[]{:T(256)} %constant.27.clone.1), padding=0_416x0_0 | pad | bytes 594946 | tf_op jit(solution)/shard_map/jit(_pad)/pad | solution.py:174
  47.0 20.6 %shard_map.139 = bf16[2,16,48,112]{3,2,1,0:T(8,128)(2,1)} custom-call(bf16[2,16,48,112]{3,2,1,0:T(8,128)(2,1)} %bitcast.81), custom_call_target="tpu_custom_call" | custom-call | tf_op jit(solution)/shard_map/pallas_call | solution.py:177
  67.7 1.0 %slice.25 = bf16[1120,112]{1,0:T(8,128)(2,1)S(1)} slice(bf16[1536,112]{1,0:T(8,128)(2,1)} %bitcast.82), slice={[0:1120], [0:112]} | slice | bytes 501760 | tf_op jit(solution)/shard_map/slice | solution.py:187
  68.6 1.2 %convolution_convert_fusion = bf16[10,112,256]{2,1,0:T(8,128)(2,1)} fusion(bf16[10,112,112]{2,1,0:T(8,128)(2,1)S(1)} %bitcast.75, bf16[256,10,112]{0,2,1:T(8,128)(2,1)S(1)} %bitcast.65), kind=kOutput, calls=%fused_computation.11 | convolution fusion | flops 64512000 | bytes 1397760 | tf_op jit(solution)/shard_map/the,hef->thf/dot_general | solution.py:264
  69.8 0.3 fusion.12
  70.1 1.0 %fusion.7 = bf16[256,1120]{0,1:T(8,128)(2,1)} fusion(f32[10,112,256]{2,1,0:T(8,128)S(1)} %fusion.12, bf16[256,1120]{0,1:T(8,128)(2,1)S(1)} %copy-done.1), kind=kLoop, calls=%fused_computation.20 | loop fusion | flops 1433600 | bytes 2293760 | tf_op jit(solution)/shard_map/convert_element_type | solution.py:256
  71.1 0.0 copy-start.2
  71.1 0.3 fusion.13
  71.4 0.8 %copy-done.2 = bf16[256,1120]{0,1:T(8,128)(2,1)S(1)} copy-done((bf16[256,1120]{0,1:T(8,128)(2,1)S(1)}, bf16[256,1120]{0,1:T(8,128)(2,1)}, u32[]{:S(2)}) %copy-start.2) | copy-done | bytes 573464
  72.2 1.1 %fusion.8 = bf16[256,1120]{0,1:T(8,128)(2,1)} fusion(f32[10,112,256]{2,1,0:T(8,128)S(1)} %fusion.13, f32[256]{0:T(256)S(1)} %and_select_fusion, bf16[256,1120]{0,1:T(8,128)(2,1)S(1)} %copy-done.2), kind=kLoop, calls=%fused_computation.22 | loop fusion | flops 1720320 | bytes 2294784 | tf_op jit(solution)/shard_map/convert_element_type | solution.py:262
  (4 shorter events, 0.0 us)
Async XLA Ops:
  0.6 1.1 %copy-start = (bf16[256,1120]{0,1:T(8,128)(2,1)S(1)}, bf16[256,1120]{0,1:T(8,128)(2,1)}, u32[]{:S(2)}) copy-start(bf16[256,1120]{0,1:T(8,128)(2,1)} %param.13) | copy-start | bytes 1720324
  4.9 1.1 %copy-start.4 = (bf16[256,1120]{0,1:T(8,128)(2,1)S(1)}, bf16[256,1120]{0,1:T(8,128)(2,1)}, u32[]{:S(2)}) copy-start(bf16[256,1120]{0,1:T(8,128)(2,1)} %param.16) | copy-start | bytes 1720324
  7.7 30.7 %copy-start.1 = (bf16[256,1120]{0,1:T(8,128)(2,1)S(1)}, bf16[256,1120]{0,1:T(8,128)(2,1)}, u32[]{:S(2)}) copy-start(bf16[256,1120]{0,1:T(8,128)(2,1)} %param.11) | copy-start | bytes 1720324
  7.7 30.7 %copy-start.3 = (bf16[256,1120]{0,1:T(8,128)(2,1)S(1)}, bf16[256,1120]{0,1:T(8,128)(2,1)}, u32[]{:S(2)}) copy-start(bf16[256,1120]{0,1:T(8,128)(2,1)} %param.14) | copy-start | bytes 1720324
  38.4 2.2 %slice-start = ((s8[5160960]{0:T(1024)(128)(4,1)}), s8[4194304]{0:T(1024)(128)(4,1)S(1)}, s32[]{:S(2)}) async-start(s8[5160960]{0:T(1024)(128)(4,1)} %bitcast.88), calls=%async_computation | async-start | bytes 8388608
  39.1 1.9 %slice-start.1 = ((s8[5160960]{0:T(1024)(128)(4,1)}), s8[966656]{0:T(1024)(128)(4,1)S(1)}, s32[]{:S(2)}) async-start(s8[5160960]{0:T(1024)(128)(4,1)} %bitcast.88), calls=%async_computation.1 | async-start | bytes 1933312
  40.0 1.5 %copy-start.5 = (bf16[256,2240]{0,1:T(8,128)(2,1)S(1)}, bf16[256,2240]{0,1:T(8,128)(2,1)}, u32[]{:S(2)}) copy-start(bf16[256,2240]{0,1:T(8,128)(2,1)} %param.17) | copy-start | bytes 3440644
  43.8 1.5 %copy-start.6 = (bf16[256,2240]{0,1:T(8,128)(2,1)}, bf16[256,2240]{0,1:T(8,128)(2,1)S(1)}, u32[]{:S(2)}) copy-start(bf16[256,2240]{0,1:T(8,128)(2,1)S(1)} %fusion) | copy-start | bytes 3440644
  71.1 1.1 %copy-start.2 = (bf16[256,1120]{0,1:T(8,128)(2,1)S(1)}, bf16[256,1120]{0,1:T(8,128)(2,1)}, u32[]{:S(2)}) copy-start(bf16[256,1120]{0,1:T(8,128)(2,1)} %param.12) | copy-start | bytes 1720324

commit v2 on v0

v2 whole, which is shorter than its diff:
```python
import functools

import jax
import jax.numpy as jnp
from jax import lax
from jax.experimental import pallas as pl
from jax.experimental.pallas import tpu as pltpu
from jax.sharding import PartitionSpec as P

H = 10
E = 112
BLK = 64


MESH = pl.DeviceIdType.MESH
LANES = 128
f32 = jnp.float32
bf16 = jnp.bfloat16


def norm_back(unnorm, scale_inv, weighted):
    inner_mean = jnp.mean(unnorm * weighted, axis=-1, keepdims=True)
    return scale_inv * weighted - unnorm * (scale_inv * scale_inv * scale_inv) * inner_mean


def dot(left, right, over):
    return lax.dot_general(left, right, ((over[:1], over[1:]), ((), ())), preferred_element_type=f32)


class Where:
    def __init__(self, chips, depth):
        seq = lax.axis_index("seq")
        self.sub = lax.axis_index("sub")
        self.depth = depth
        self.chips = chips
        self.core = lax.rem(seq, 2)
        self.chip = (seq // 2) * depth + self.sub
        self.partner = (seq + 1 - 2 * self.core, self.sub)

    def peer(self, index):
        return (index // self.depth) * 2 + self.core, lax.rem(index, self.depth)

    def ahead(self, step):
        return lax.rem(self.chip + step, self.chips)

    def behind(self, step):
        return lax.rem(self.chip + self.chips - step, self.chips)


def greet(at):
    barrier = pltpu.get_barrier_semaphore()
    pl.semaphore_signal(barrier, inc=1, device_id=at.partner, device_id_type=MESH)

    @pl.loop(1, at.chips)
    def _(step):
        pl.semaphore_signal(
            barrier, inc=1, device_id=at.peer(at.ahead(step)), device_id_type=MESH
        )


def all_total(at, piece, wide, near, sent, out, half, mine, parts, sems, between=None):
    s0, r0, s1, r1, s2, r2, s3, r3 = sems
    core, chip, chips = at.core, at.chip, at.chips

    def copy(src, dst, send, recv, to):
        return pltpu.make_async_remote_copy(
            src_ref=src,
            dst_ref=dst,
            send_sem=send,
            recv_sem=recv,
            device_id=to,
            device_id_type=MESH,
        )

    def rows(index, side=None):
        base = index if side is None else side * chips + index
        return pl.ds(pl.multiple_of(base * piece, 16), piece)

    def scatter(index, slot):
        return copy(
            mine.at[rows(index)], parts.at[rows(slot)], s1.at[index], r1.at[slot], at.peer(index)
        )

    def gather(index, slot):
        return copy(
            out.at[rows(chip, core)],
            out.at[rows(slot, core)],
            s2.at[index],
            r2.at[slot],
            at.peer(index),
        )

    def forward(index, side):
        return copy(
            out.at[rows(index, core)],
            out.at[rows(index, side)],
            s3.at[index],
            r3.at[index],
            at.partner,
        )

    size = wide.shape[0]
    for block in range(wide.shape[1] // LANES):
        lanes = wide[:, block * LANES : (block + 1) * LANES]
        near[block * size : (block + 1) * size, :] = lanes
        sent[block * size : (block + 1) * size, :] = lanes.astype(bf16)
    used = size * (wide.shape[1] // LANES)
    if used < near.shape[0]:
        near[used:, :] = jnp.zeros((near.shape[0] - used, LANES), f32)
        sent[used:, :] = jnp.zeros((near.shape[0] - used, LANES), bf16)

    other = pl.ds(pl.multiple_of((1 - core) * (chips * piece), 16), chips * piece)
    swap = copy(sent.at[other], half, s0, r0, at.partner)
    swap.start()
    if between is not None:
        between()
    swap.wait()

    def pair(index):
        return near[rows(index, core), :] + half[rows(index), :].astype(f32)

    @pl.loop(1, chips)
    def _(step):
        index = at.ahead(step)
        mine[rows(index), :] = pair(index).astype(bf16)
        scatter(index, chip).start()

    def add(step, acc):
        index = at.behind(step)
        scatter(index, index).wait_recv()
        return acc + parts[rows(index), :].astype(f32)

    out[rows(chip, core), :] = lax.fori_loop(1, chips, add, pair(chip)).astype(bf16)

    @pl.loop(1, chips)
    def _(step):
        gather(at.ahead(step), chip).start()

    forward(chip, core).start()

    @pl.loop(1, chips)
    def _(step):
        index = at.behind(step)
        gather(index, index).wait_recv()
        forward(index, core).start()

    @pl.loop(1, chips)
    def _(step):
        index = at.ahead(step)
        scatter(index, chip).wait_send()
        gather(index, chip).wait_send()

    @pl.loop(0, chips)
    def _(step):
        index = at.behind(step)
        forward(index, 1 - core).wait_recv()
        forward(index, core).wait_send()

    for block in range(wide.shape[1] // LANES):
        wide[:, block * LANES : (block + 1) * LANES] = out[
            block * size : (block + 1) * size, :
        ].astype(f32)


def step_kernel(
    chips, depth, pieces,
    q_hbm, k_hbm, v_hbm, qt_hbm, kt_hbm, vt_hbm, t_hbm, w_hbm, gain_ref, clip_ref, flags_ref,
    res_ref, gq_ref, gk_ref, gv_ref,
    q, k, v, qt, kt, vt, teach, weight, loads,
    wide1, near1, sent1, out1, half1, mine1, parts1,
    wide2, near2, sent2, out2, half2, mine2, parts2,
    unnorm, scale, normed, ngrad, ugrad,
    *sems,
):
    at = Where(chips, depth)
    tok = q.shape[0]
    incoming = [
        pltpu.make_async_copy(src, dst, loads.at[i])
        for i, (src, dst) in enumerate(
            [
                (k_hbm, k),
                (v_hbm, v),
                (kt_hbm, kt),
                (vt_hbm, vt),
                (q_hbm, q),
                (qt_hbm, qt),
                (w_hbm, weight),
                (t_hbm, teach),
            ]
        )
    ]
    greet(at)
    for load in incoming:
        load.start()

    rowid = lax.broadcasted_iota(jnp.int32, (tok, E), 0)
    device = lax.axis_index("seq") * depth + at.sub
    kept = jnp.zeros((tok, E), jnp.int32)
    for block in range(tok // BLK):
        inside = (rowid >= block * BLK) & (rowid < (block + 1) * BLK)
        kept = jnp.where(inside, flags_ref[block], kept)
    before = rowid + device * tok < clip_ref[0]
    valid = jnp.where(before & (kept == 1), 1.0, 0.0).astype(f32)

    def head(ref, h):
        return ref[:, h * E : (h + 1) * E]

    def key_parts(h):
        keys = head(k, h).astype(f32)
        slope = jnp.where(keys > 0, valid, 0.0)
        return jnp.maximum(keys, 0.0) * valid, slope

    for load in incoming[:4]:
        load.wait()
    edge = wide1.shape[1] - LANES
    wide1[:, edge:] = jnp.zeros((wide1.shape[0], LANES), f32)
    wide2[:, edge:] = jnp.zeros((wide2.shape[0], LANES), f32)
    for h in range(H):
        feat, slope = key_parts(h)
        feat = feat.astype(bf16)
        along = (slope * head(kt, h).astype(f32)).astype(bf16)
        vals = head(v, h)
        cols = slice(h * E, (h + 1) * E)
        wide1[:E, cols] = dot(feat, vals, (0, 0))
        wide1[E:, cols] = dot(along, vals, (0, 0)) + dot(feat, head(vt, h), (0, 0))

    pl.semaphore_wait(pltpu.get_barrier_semaphore(), chips)
    all_total(
        at, pieces[0], wide1, near1, sent1, out1, half1, mine1, parts1, sems[:8]
    )

    for load in incoming[4:]:
        load.wait()

    def state(h):
        return head(wide1, h)[:E].astype(bf16)

    def query(h):
        rows = head(q, h).astype(f32)
        return jnp.maximum(rows, 0.0).astype(bf16), jnp.where(rows > 0, 1.0, 0.0).astype(f32)

    for h in range(H):
        both = head(wide1, h).astype(bf16)
        feat, slope = query(h)
        along = (slope * head(qt, h).astype(f32)).astype(bf16)
        un = dot(feat, both[:E], (1, 0))
        un_dot = dot(along, both[:E], (1, 0)) + dot(feat, both[E:], (1, 0))
        inv = lax.rsqrt(jnp.mean(un * un, axis=-1, keepdims=True) + 1e-06)
        unnorm[h] = un
        scale[h] = inv
        normed[:, h * E : (h + 1) * E] = head(gain_ref, h) * norm_back(un, inv, un_dot)

    velocity = dot(normed[...].astype(bf16), weight[...], (1, 0))
    residual = (velocity - teach[...].astype(f32)).astype(bf16)
    res_ref[...] = residual
    ngrad[...] = dot(residual, weight[...], (1, 1))
    for h in range(H):
        weighted = head(gain_ref, h) * head(ngrad, h)
        grad = norm_back(unnorm[h], scale[h], weighted).astype(bf16)
        ugrad[h] = grad
        wide2[:, h * E : (h + 1) * E] = dot(query(h)[0], grad, (0, 0))

    def query_grads():
        for h in range(H):
            back = dot(ugrad[h], state(h), (1, 1))
            gq_ref[:, h * E : (h + 1) * E] = (query(h)[1] * back).astype(bf16)

    all_total(
        at, pieces[1], wide2, near2, sent2, out2, half2, mine2, parts2, sems[8:], query_grads
    )

    for h in range(H):
        total = head(wide2, h).astype(bf16)
        feat, slope = key_parts(h)
        cols = slice(h * E, (h + 1) * E)
        gk_ref[:, cols] = (slope * dot(head(v, h), total, (1, 1))).astype(bf16)
        gv_ref[:, cols] = dot(feat.astype(bf16), total, (1, 0)).astype(bf16)


def local(
    query_rows,
    key_rows,
    value_rows,
    query_tangent,
    key_tangent,
    value_tangent,
    teacher,
    out_weight,
    norm_gain,
    clip_length,
    block_mask,
):
    tok, width = query_rows.shape
    depth = lax.axis_size("sub")
    chips = lax.axis_size("seq") // 2 * depth
    padded = -(-width // LANES) * LANES
    vmem = pltpu.VMEM
    dma = pltpu.SemaphoreType.DMA
    pieces = []
    totals = []
    for size in (2 * E, E):
        piece = -(-(size * padded // LANES) // (32 * chips)) * 16
        pieces.append(piece)
        half = (chips * piece, LANES)
        full = (2 * chips * piece, LANES)
        totals += [vmem((size, padded), f32), vmem(full, f32), vmem(full, bf16), vmem(full, bf16)]
        totals += [vmem(half, bf16)] * 3
    arrays = (query_rows, key_rows, value_rows, query_tangent, key_tangent, value_tangent)
    arrays += (teacher, out_weight)
    anywhere = pl.BlockSpec(memory_space=pl.ANY)
    in_vmem = pl.BlockSpec(memory_space=vmem)
    in_smem = pl.BlockSpec(memory_space=pltpu.SMEM)
    return pl.pallas_call(
        functools.partial(step_kernel, chips, depth, pieces),
        out_shape=(
            jax.ShapeDtypeStruct(teacher.shape, bf16),
            jax.ShapeDtypeStruct(query_rows.shape, bf16),
            jax.ShapeDtypeStruct(query_rows.shape, bf16),
            jax.ShapeDtypeStruct(query_rows.shape, bf16),
        ),
        in_specs=[anywhere] * 8 + [in_vmem, in_smem, in_smem],
        out_specs=[in_vmem] * 4,
        scratch_shapes=[vmem(array.shape, array.dtype) for array in arrays]
        + [dma((8,))]
        + totals
        + [
            vmem((H, tok, E), f32),
            vmem((H, tok, 1), f32),
            vmem((tok, width), f32),
            vmem((tok, width), f32),
            vmem((H, tok, E), bf16),
        ]
        + ([dma, dma] + [dma((chips,))] * 6) * 2,
        compiler_params=pltpu.CompilerParams(collective_id=0, has_side_effects=True),
    )(*arrays, norm_gain[None, :], clip_length, block_mask)


def solution(mesh):
    return jax.shard_map(
        local,
        mesh=mesh,
        in_specs=(
            P(("seq", "sub"), None),
            P(("seq", "sub"), None),
            P(("seq", "sub"), None),
            P(("seq", "sub"), None),
            P(("seq", "sub"), None),
            P(("seq", "sub"), None),
            P(("seq", "sub"), None),
            P(),
            P(),
            P(),
            P(("seq", "sub")),
        ),
        out_specs=(
            P(("seq", "sub"), None),
            P(("seq", "sub"), None),
            P(("seq", "sub"), None),
            P(("seq", "sub"), None),
        ),
        check_vma=False,
    )
```

time: 120 us -> 76.1 us (0.63)
  blocking collectives: 99.8 us -> 0 us
  Pallas kernels: 0 us -> 58.5 us
  local copies, waits for them, and re-layouts: 3.56 us -> 15.9 us
  matrix products: 7.92 us -> 0 us
  other arithmetic: 7.01 us -> 0 us
    psum x2 -> x0, blocking collectives: 99.8 us -> none  [combine_states(): totals = lax.psum(stacked, ('seq', 'sub'))]
    pallas_call x0 -> x1, Pallas kernels: none -> 58.5 us  [local(): pl.pallas_call(functools.partial(step_kernel, chips, depth, pieces), out_...]
    dot_general x12 -> x0, matrix products: 7.92 us -> none  [the longest x1 2.33 us: local(): velocity = jnp.dot(normed_dot, out_weight, preferred_element_type=f32)]
    unnamed x16 -> x25, local copies, waits for them, and re-layouts: 2.62 us -> 8.98 us
    convert_element_type x6 -> x0, other arithmetic: 6 us -> none  [the longest x1 1.63 us: local(): key_feat = (valid_rows * jnp.maximum(key_vals, 0.0)).astype(bf16)]
    pallas_call x0 -> x4, local copies, waits for them, and re-layouts: none -> 5.61 us  [local(): pl.pallas_call(functools.partial(step_kernel, chips, depth, pieces), out_...]
    broadcast_in_dim x1, local copies, waits for them, and re-layouts: 0.08 us -> 1.29 us  [local(): norm_gain[None, :]]
where the time goes in v2:
time: 76.1 us; the launch traced here: 75.8 us
  Pallas kernels  58.5 us (77%)
  local copies, waits for them, and re-layouts  15.9 us (21%)
  between operations  1.42 us (2%)
    pallas_call x1, Pallas kernels, local(): pl.pallas_call(functools.partial(step_kernel, chips, depth, pieces), out_...  58.5 us
    unnamed x25, local copies, waits for them, and re-layouts  8.98 us
    pallas_call x4, local copies, waits for them, and re-layouts, local(): pl.pallas_call(functools.partial(step_kernel, chips, depth, pieces), out_...  5.61 us

profile of v2, /device:TPU:0, one launch (start us, length us, event | category | flops | bytes accessed | tf_op | source)
XLA Modules:
  0.0 75.8 jit_solution(17810516264473059293)
XLA Ops:
  0.6 0.0 copy-start.5
  0.6 0.0 copy-start.4
  1.4 1.3 %broadcast_in_dim.3.gain_ref = f32[1,1120]{1,0:T(1,128)} reshape(f32[1120]{0:T(1024)} %param.19) | data formatting | bytes 8960 | tf_op jit(solution)/shard_map/broadcast_in_dim | solution.py:335
  2.7 2.1 %copy.15.q_hbm = bf16[256,1120]{1,0:T(8,128)(2,1)} copy(bf16[256,1120]{0,1:T(8,128)(2,1)} %param.11) | data formatting | bytes 1146880 | tf_op args[0]
  4.8 0.0 copy-done.4
  4.8 0.0 copy-start.6
  4.8 1.1 %copy.16.k_hbm = bf16[256,1120]{1,0:T(8,128)(2,1)} copy(bf16[256,1120]{0,1:T(8,128)(2,1)S(1)} %copy-done.4) | data formatting | bytes 1146880 | tf_op args[1]
  5.9 0.0 copy-done.5
  5.9 0.0 copy-start.7
  5.9 1.1 %copy.17.v_hbm = bf16[256,1120]{1,0:T(8,128)(2,1)} copy(bf16[256,1120]{0,1:T(8,128)(2,1)S(1)} %copy-done.5) | data formatting | bytes 1146880 | tf_op args[2]
  6.9 0.0 copy-done.6
  6.9 0.0 copy-start.8
  6.9 1.1 %copy.18.qt_hbm = bf16[256,1120]{1,0:T(8,128)(2,1)} copy(bf16[256,1120]{0,1:T(8,128)(2,1)S(1)} %copy-done.6) | data formatting | bytes 1146880 | tf_op args[3]
  8.0 0.0 copy-done.7
  8.0 0.0 copy-start
  8.0 1.1 %copy.19.kt_hbm = bf16[256,1120]{1,0:T(8,128)(2,1)} copy(bf16[256,1120]{0,1:T(8,128)(2,1)S(1)} %copy-done.7) | data formatting | bytes 1146880 | tf_op args[4]
  9.1 0.0 copy-done.8
  9.1 1.1 %copy.20.vt_hbm = bf16[256,1120]{1,0:T(8,128)(2,1)} copy(bf16[256,1120]{0,1:T(8,128)(2,1)S(1)} %copy-done.8) | data formatting | bytes 1146880 | tf_op args[5]
  10.1 0.0 copy-done
  10.1 1.5 %copy.21.t_hbm = bf16[256,2240]{1,0:T(8,128)(2,1)} copy(bf16[256,2240]{0,1:T(8,128)(2,1)S(1)} %copy-done) | data formatting | bytes 2293760 | tf_op args[6]
  11.7 58.5 %shard_map.138 = (bf16[256,2240]{1,0:T(8,128)(2,1)}, bf16[256,1120]{1,0:T(8,128)(2,1)}, bf16[256,1120]{1,0:T(8,128)(2,1)}, bf16[256,1120]{1,0:T(8,128)(2,1)}) custom-call(bf16[256,1120]{1,0:T(8,128)(2,1)} %copy.15.q_hbm, bf16[256,1120]{1,0:T(8,128)(2,1)} %copy.16.k_hbm, bf16[256,1120]{1,0:T(8,128)(2,1)} %copy.17.v_hbm, bf16[256,1120]{1,0:T(8,128)(2,1)} %copy.18.qt_hbm, ...), custom_call_target="tpu_custom_call" | custom-call | tf_op jit(solution)/shard_map/pallas_call | solution.py:313
  70.2 0.0 copy-start.3
  70.2 0.0 copy-start.2
  70.2 2.5 %copy.22 = bf16[256,2240]{0,1:T(8,128)(2,1)} copy(bf16[256,2240]{1,0:T(8,128)(2,1)} %get-tuple-element.4) | data formatting | bytes 2293760 | tf_op jit(solution)/shard_map/pallas_call | solution.py:313
  72.7 0.0 copy-done.3
  72.7 0.0 copy-start.1
  72.7 1.1 %copy.23 = bf16[256,1120]{0,1:T(8,128)(2,1)} copy(bf16[256,1120]{1,0:T(8,128)(2,1)S(1)} %copy-done.3) | data formatting | bytes 1146880 | tf_op jit(solution)/shard_map/pallas_call | solution.py:313
  73.7 0.0 copy-done.2
  73.7 1.1 %copy.24 = bf16[256,1120]{0,1:T(8,128)(2,1)} copy(bf16[256,1120]{1,0:T(8,128)(2,1)S(1)} %copy-done.2) | data formatting | bytes 1146880 | tf_op jit(solution)/shard_map/pallas_call | solution.py:313
  74.8 0.0 copy-done.1
  74.8 1.1 %copy.25 = bf16[256,1120]{0,1:T(8,128)(2,1)} copy(bf16[256,1120]{1,0:T(8,128)(2,1)S(1)} %copy-done.1) | data formatting | bytes 1146880 | tf_op jit(solution)/shard_map/pallas_call | solution.py:313
Async XLA Ops:
  0.6 5.2 %copy-start.5 = (bf16[256,1120]{0,1:T(8,128)(2,1)S(1)}, bf16[256,1120]{0,1:T(8,128)(2,1)}, u32[]{:S(2)}) copy-start(bf16[256,1120]{0,1:T(8,128)(2,1)} %param.13) | copy-start | bytes 1720324
  0.6 4.2 %copy-start.4 = (bf16[256,1120]{0,1:T(8,128)(2,1)S(1)}, bf16[256,1120]{0,1:T(8,128)(2,1)}, u32[]{:S(2)}) copy-start(bf16[256,1120]{0,1:T(8,128)(2,1)} %param.12) | copy-start | bytes 1720324
  4.8 2.1 %copy-start.6 = (bf16[256,1120]{0,1:T(8,128)(2,1)S(1)}, bf16[256,1120]{0,1:T(8,128)(2,1)}, u32[]{:S(2)}) copy-start(bf16[256,1120]{0,1:T(8,128)(2,1)} %param.14) | copy-start | bytes 1720324
  5.9 2.1 %copy-start.7 = (bf16[256,1120]{0,1:T(8,128)(2,1)S(1)}, bf16[256,1120]{0,1:T(8,128)(2,1)}, u32[]{:S(2)}) copy-start(bf16[256,1120]{0,1:T(8,128)(2,1)} %param.15) | copy-start | bytes 1720324
  6.9 2.1 %copy-start.8 = (bf16[256,1120]{0,1:T(8,128)(2,1)S(1)}, bf16[256,1120]{0,1:T(8,128)(2,1)}, u32[]{:S(2)}) copy-start(bf16[256,1120]{0,1:T(8,128)(2,1)} %param.16) | copy-start | bytes 1720324
  8.0 2.1 %copy-start = (bf16[256,2240]{0,1:T(8,128)(2,1)S(1)}, bf16[256,2240]{0,1:T(8,128)(2,1)}, u32[]{:S(2)}) copy-start(bf16[256,2240]{0,1:T(8,128)(2,1)} %param.17) | copy-start | bytes 3440644
  70.2 2.5 %copy-start.3 = (bf16[256,1120]{1,0:T(8,128)(2,1)S(1)}, bf16[256,1120]{1,0:T(8,128)(2,1)}, u32[]{:S(2)}) copy-start(bf16[256,1120]{1,0:T(8,128)(2,1)} %get-tuple-element.5) | copy-start | bytes 1720324
  70.2 3.5 %copy-start.2 = (bf16[256,1120]{1,0:T(8,128)(2,1)S(1)}, bf16[256,1120]{1,0:T(8,128)(2,1)}, u32[]{:S(2)}) copy-start(bf16[256,1120]{1,0:T(8,128)(2,1)} %get-tuple-element.6) | copy-start | bytes 1720324
  72.7 2.1 %copy-start.1 = (bf16[256,1120]{1,0:T(8,128)(2,1)S(1)}, bf16[256,1120]{1,0:T(8,128)(2,1)}, u32[]{:S(2)}) copy-start(bf16[256,1120]{1,0:T(8,128)(2,1)} %get-tuple-element.7) | copy-start | bytes 1720324

commit v3 on v2

--- a/solution.py
+++ b/solution.py
@@ -19,7 +19,7 @@
 
 
 def norm_back(unnorm, scale_inv, weighted):
-    inner_mean = jnp.mean(unnorm * weighted, axis=-1, keepdims=True)
+    inner_mean = jnp.mean(unnorm * weighted, axis=0, keepdims=True)
     return scale_inv * weighted - unnorm * (scale_inv * scale_inv * scale_inv) * inner_mean
 
 
@@ -58,7 +58,7 @@
         )
 
 
-def all_total(at, piece, wide, near, sent, out, half, mine, parts, sems, between=None):
+def all_total(at, piece, wide, near, sent, out, half, mine, parts, sems, between=None, after=None):
     s0, r0, s1, r1, s2, r2, s3, r3 = sems
     core, chip, chips = at.core, at.chip, at.chips
 
@@ -125,6 +125,9 @@
         mine[rows(index), :] = pair(index).astype(bf16)
         scatter(index, chip).start()
 
+    if after is not None:
+        after()
+
     def add(step, acc):
         index = at.behind(step)
         scatter(index, index).wait_recv()
@@ -169,11 +172,11 @@
     q, k, v, qt, kt, vt, teach, weight, loads,
     wide1, near1, sent1, out1, half1, mine1, parts1,
     wide2, near2, sent2, out2, half2, mine2, parts2,
-    unnorm, scale, normed, ngrad, ugrad,
+    unnorm, scale, normed, ngrad, ugrad, turned, gain,
     *sems,
 ):
     at = Where(chips, depth)
-    tok = q.shape[0]
+    tok = q.shape[1]
     incoming = [
         pltpu.make_async_copy(src, dst, loads.at[i])
         for i, (src, dst) in enumerate(
@@ -182,9 +185,9 @@
                 (v_hbm, v),
                 (kt_hbm, kt),
                 (vt_hbm, vt),
+                (w_hbm, weight),
                 (q_hbm, q),
                 (qt_hbm, qt),
-                (w_hbm, weight),
                 (t_hbm, teach),
             ]
         )
@@ -193,88 +196,98 @@
     for load in incoming:
         load.start()
 
-    rowid = lax.broadcasted_iota(jnp.int32, (tok, E), 0)
+    token = lax.broadcasted_iota(jnp.int32, (8, tok), 1)
     device = lax.axis_index("seq") * depth + at.sub
-    kept = jnp.zeros((tok, E), jnp.int32)
+    kept = jnp.zeros((8, tok), jnp.int32)
     for block in range(tok // BLK):
-        inside = (rowid >= block * BLK) & (rowid < (block + 1) * BLK)
+        inside = (token >= block * BLK) & (token < (block + 1) * BLK)
         kept = jnp.where(inside, flags_ref[block], kept)
-    before = rowid + device * tok < clip_ref[0]
-    valid = jnp.where(before & (kept == 1), 1.0, 0.0).astype(f32)
+    before = token + device * tok < clip_ref[0]
+    valid = jnp.where(before & (kept == 1), 1.0, 0.0).astype(f32)[:1]
 
     def head(ref, h):
-        return ref[:, h * E : (h + 1) * E]
+        return ref[h * E : (h + 1) * E, :]
+
+    def square(ref, h):
+        return ref[:, h * E : (h + 1) * E].astype(bf16)
 
     def key_parts(h):
         keys = head(k, h).astype(f32)
-        slope = jnp.where(keys > 0, valid, 0.0)
+        slope = jnp.where(keys > 0, 1.0, 0.0) * valid
         return jnp.maximum(keys, 0.0) * valid, slope
 
-    for load in incoming[:4]:
-        load.wait()
     edge = wide1.shape[1] - LANES
     wide1[:, edge:] = jnp.zeros((wide1.shape[0], LANES), f32)
     wide2[:, edge:] = jnp.zeros((wide2.shape[0], LANES), f32)
+    for load in incoming[:4]:
+        load.wait()
     for h in range(H):
         feat, slope = key_parts(h)
         feat = feat.astype(bf16)
         along = (slope * head(kt, h).astype(f32)).astype(bf16)
         vals = head(v, h)
         cols = slice(h * E, (h + 1) * E)
-        wide1[:E, cols] = dot(feat, vals, (0, 0))
-        wide1[E:, cols] = dot(along, vals, (0, 0)) + dot(feat, head(vt, h), (0, 0))
+        wide1[:E, cols] = dot(vals, feat, (1, 1))
+        wide1[E:, cols] = dot(vals, along, (1, 1)) + dot(head(vt, h), feat, (1, 1))
+
+    def prepare():
+        row = lax.broadcasted_iota(jnp.int32, (E, E), 0)
+        col = lax.broadcasted_iota(jnp.int32, (E, E), 1)
+        for h in range(H):
+            spread = jnp.where(row == col, gain_ref[:, h * E : (h + 1) * E], 0.0)
+            gain[h * E : (h + 1) * E, :] = jnp.sum(spread, axis=1, keepdims=True)
+        for load in incoming[4:]:
+            load.wait()
+        for start in range(0, weight.shape[1], 256):
+            stop = min(start + 256, weight.shape[1])
+            turned[start:stop, :] = weight[:, start:stop].T
 
     pl.semaphore_wait(pltpu.get_barrier_semaphore(), chips)
     all_total(
-        at, pieces[0], wide1, near1, sent1, out1, half1, mine1, parts1, sems[:8]
+        at, pieces[0], wide1, near1, sent1, out1, half1, mine1, parts1, sems[:8], None, prepare
     )
-
-    for load in incoming[4:]:
-        load.wait()
-
-    def state(h):
-        return head(wide1, h)[:E].astype(bf16)
 
     def query(h):
         rows = head(q, h).astype(f32)
         return jnp.maximum(rows, 0.0).astype(bf16), jnp.where(rows > 0, 1.0, 0.0).astype(f32)
 
     for h in range(H):
-        both = head(wide1, h).astype(bf16)
+        rows = slice(h * E, (h + 1) * E)
+        both = square(wide1, h)
         feat, slope = query(h)
         along = (slope * head(qt, h).astype(f32)).astype(bf16)
-        un = dot(feat, both[:E], (1, 0))
-        un_dot = dot(along, both[:E], (1, 0)) + dot(feat, both[E:], (1, 0))
-        inv = lax.rsqrt(jnp.mean(un * un, axis=-1, keepdims=True) + 1e-06)
-        unnorm[h] = un
+        un = dot(both[:E], feat, (1, 0))
+        un_dot = dot(both[:E], along, (1, 0)) + dot(both[E:], feat, (1, 0))
+        inv = lax.rsqrt(jnp.mean(un * un, axis=0, keepdims=True) + 1e-06)
+        unnorm[rows, :] = un
         scale[h] = inv
-        normed[:, h * E : (h + 1) * E] = head(gain_ref, h) * norm_back(un, inv, un_dot)
-
-    velocity = dot(normed[...].astype(bf16), weight[...], (1, 0))
-    residual = (velocity - teach[...].astype(f32)).astype(bf16)
-    res_ref[...] = residual
-    ngrad[...] = dot(residual, weight[...], (1, 1))
+        normed[rows, :] = (gain[rows, :] * norm_back(un, inv, un_dot)).astype(bf16)
+
+    velocity = dot(turned[...], normed[...], (1, 0))
+    res_ref[...] = (velocity - teach[...].astype(f32)).astype(bf16)
+    ngrad[...] = dot(weight[...], res_ref[...], (1, 0))
     for h in range(H):
-        weighted = head(gain_ref, h) * head(ngrad, h)
-        grad = norm_back(unnorm[h], scale[h], weighted).astype(bf16)
-        ugrad[h] = grad
-        wide2[:, h * E : (h + 1) * E] = dot(query(h)[0], grad, (0, 0))
+        rows = slice(h * E, (h + 1) * E)
+        weighted = gain[rows, :] * head(ngrad, h)
+        grad = norm_back(head(unnorm, h), scale[h], weighted).astype(bf16)
+        ugrad[rows, :] = grad
+        wide2[:, h * E : (h + 1) * E] = dot(grad, query(h)[0], (1, 1))
 
     def query_grads():
         for h in range(H):
-            back = dot(ugrad[h], state(h), (1, 1))
-            gq_ref[:, h * E : (h + 1) * E] = (query(h)[1] * back).astype(bf16)
+            back = dot(square(wide1, h)[:E], head(ugrad, h), (0, 0))
+            gq_ref[h * E : (h + 1) * E, :] = (query(h)[1] * back).astype(bf16)
 
     all_total(
-        at, pieces[1], wide2, near2, sent2, out2, half2, mine2, parts2, sems[8:], query_grads
+        at, pieces[1], wide2, near2, sent2, out2, half2, mine2, parts2, sems[8:], None, query_grads
     )
 
     for h in range(H):
-        total = head(wide2, h).astype(bf16)
+        total = square(wide2, h)
         feat, slope = key_parts(h)
-        cols = slice(h * E, (h + 1) * E)
-        gk_ref[:, cols] = (slope * dot(head(v, h), total, (1, 1))).astype(bf16)
-        gv_ref[:, cols] = dot(feat.astype(bf16), total, (1, 0)).astype(bf16)
+        rows = slice(h * E, (h + 1) * E)
+        gk_ref[rows, :] = (slope * dot(total, head(v, h), (0, 0))).astype(bf16)
+        gv_ref[rows, :] = dot(total, feat.astype(bf16), (1, 0)).astype(bf16)
 
 
 def local(
@@ -306,17 +319,17 @@
         totals += [vmem((size, padded), f32), vmem(full, f32), vmem(full, bf16), vmem(full, bf16)]
         totals += [vmem(half, bf16)] * 3
     arrays = (query_rows, key_rows, value_rows, query_tangent, key_tangent, value_tangent)
-    arrays += (teacher, out_weight)
+    arrays = tuple(array.T for array in arrays + (teacher,)) + (out_weight,)
     anywhere = pl.BlockSpec(memory_space=pl.ANY)
     in_vmem = pl.BlockSpec(memory_space=vmem)
     in_smem = pl.BlockSpec(memory_space=pltpu.SMEM)
-    return pl.pallas_call(
+    outs = pl.pallas_call(
         functools.partial(step_kernel, chips, depth, pieces),
         out_shape=(
-            jax.ShapeDtypeStruct(teacher.shape, bf16),
-            jax.ShapeDtypeStruct(query_rows.shape, bf16),
-            jax.ShapeDtypeStruct(query_rows.shape, bf16),
-            jax.ShapeDtypeStruct(query_rows.shape, bf16),
+            jax.ShapeDtypeStruct(teacher.shape[::-1], bf16),
+            jax.ShapeDtypeStruct((width, tok), bf16),
+            jax.ShapeDtypeStruct((width, tok), bf16),
+            jax.ShapeDtypeStruct((width, tok), bf16),
         ),
         in_specs=[anywhere] * 8 + [in_vmem, in_smem, in_smem],
         out_specs=[in_vmem] * 4,
@@ -324,15 +337,18 @@
         + [dma((8,))]
         + totals
         + [
-            vmem((H, tok, E), f32),
-            vmem((H, tok, 1), f32),
-            vmem((tok, width), f32),
-            vmem((tok, width), f32),
-            vmem((H, tok, E), bf16),
+            vmem((width, tok), f32),
+            vmem((H, 1, tok), f32),
+            vmem((width, tok), bf16),
+            vmem((width, tok), f32),
+            vmem((width, tok), bf16),
+            vmem(out_weight.shape[::-1], bf16),
+            vmem((width, 1), f32),
         ]
         + ([dma, dma] + [dma((chips,))] * 6) * 2,
         compiler_params=pltpu.CompilerParams(collective_id=0, has_side_effects=True),
     )(*arrays, norm_gain[None, :], clip_length, block_mask)
+    return tuple(out.T for out in outs)
 
 
 def solution(mesh):

time: 76.1 us -> 55.5 us (0.73)
  Pallas kernels: 58.5 us -> 47.4 us
  local copies, waits for them, and re-layouts: 15.9 us -> 6.58 us
    pallas_call x1, Pallas kernels: 58.5 us -> 47.4 us  [local(): pl.pallas_call(functools.partial(step_kernel, chips, depth, pieces), out_...]
    pallas_call x4 -> x0, local copies, waits for them, and re-layouts: 5.61 us -> none  [local(): pl.pallas_call(functools.partial(step_kernel, chips, depth, pieces), out_...]
    unnamed x25 -> x10, local copies, waits for them, and re-layouts: 8.98 us -> 5.28 us
where the time goes in v3:
time: 55.5 us; the launch traced here: 55.3 us
  Pallas kernels  47.4 us (85%)
  local copies, waits for them, and re-layouts  6.58 us (12%)
  between operations  1.3 us (2%)
    pallas_call x1, Pallas kernels, local(): pl.pallas_call(functools.partial(step_kernel, chips, depth, pieces), out_...  47.4 us
    unnamed x10, local copies, waits for them, and re-layouts  5.28 us
    broadcast_in_dim x1, local copies, waits for them, and re-layouts, local(): norm_gain[None, :]  1.29 us

profile of v3, /device:TPU:0, one launch (start us, length us, event | category | flops | bytes accessed | tf_op | source)
XLA Modules:
  0.0 55.3 jit_solution(3875930692306598110)
XLA Ops:
  1.3 1.3 %broadcast_in_dim.3.gain_ref = f32[1,1120]{1,0:T(1,128)} reshape(f32[1120]{0:T(1024)} %param.19) | data formatting | bytes 8960 | tf_op jit(solution)/shard_map/broadcast_in_dim | solution.py:350
  2.6 47.4 %shard_map.138 = (bf16[2240,256]{1,0:T(8,128)(2,1)}, bf16[1120,256]{1,0:T(8,128)(2,1)}, bf16[1120,256]{1,0:T(8,128)(2,1)}, bf16[1120,256]{1,0:T(8,128)(2,1)}) custom-call(bf16[1120,256]{1,0:T(8,128)(2,1)} %bitcast.13, bf16[1120,256]{1,0:T(8,128)(2,1)} %bitcast.14, bf16[1120,256]{1,0:T(8,128)(2,1)} %bitcast.15, bf16[1120,256]{1,0:T(8,128)(2,1)} %bitcast.16, ...), custom_call_target="tpu_custom_call" | custom-call | tf_op jit(solution)/shard_map/pallas_call | solution.py:326
  50.0 0.0 copy-start.2
  50.0 2.4 %copy.20 = bf16[256,2240]{0,1:T(8,128)(2,1)} copy(bf16[256,2240]{0,1:T(8,128)(2,1)} %bitcast.12) | data formatting | bytes 2293760
  52.4 0.0 copy-done.2
  52.4 0.0 copy-start.1
  52.4 0.0 copy-start
  52.4 0.8 %copy.21 = bf16[256,1120]{0,1:T(8,128)(2,1)} copy(bf16[256,1120]{0,1:T(8,128)(2,1)S(1)} %bitcast.21) | data formatting | bytes 1146880
  53.2 0.5 copy-done.1
  53.7 0.8 %copy.22 = bf16[256,1120]{0,1:T(8,128)(2,1)} copy(bf16[256,1120]{0,1:T(8,128)(2,1)S(1)} %bitcast.20) | data formatting | bytes 1146880
  54.5 0.0 copy-done
  54.5 0.8 %copy.23 = bf16[256,1120]{0,1:T(8,128)(2,1)} copy(bf16[256,1120]{0,1:T(8,128)(2,1)S(1)} %bitcast.19) | data formatting | bytes 1146880
Async XLA Ops:
  50.0 2.4 %copy-start.2 = (bf16[1120,256]{1,0:T(8,128)(2,1)S(1)}, bf16[1120,256]{1,0:T(8,128)(2,1)}, u32[]{:S(2)}) copy-start(bf16[1120,256]{1,0:T(8,128)(2,1)} %get-tuple-element.9) | copy-start | bytes 1720324
  52.4 1.3 %copy-start.1 = (bf16[1120,256]{1,0:T(8,128)(2,1)S(1)}, bf16[1120,256]{1,0:T(8,128)(2,1)}, u32[]{:S(2)}) copy-start(bf16[1120,256]{1,0:T(8,128)(2,1)} %get-tuple-element.10) | copy-start | bytes 1720324
  52.4 2.1 %copy-start = (bf16[1120,256]{1,0:T(8,128)(2,1)S(1)}, bf16[1120,256]{1,0:T(8,128)(2,1)}, u32[]{:S(2)}) copy-start(bf16[1120,256]{1,0:T(8,128)(2,1)} %get-tuple-element.11) | copy-start | bytes 1720324

commit v4 on v3

--- a/solution.py
+++ b/solution.py
@@ -165,14 +165,24 @@
         ].astype(f32)
 
 
+def kept_tokens(tok, first, clip_ref, flags_ref):
+    token = lax.broadcasted_iota(jnp.int32, (8, tok), 1)
+    kept = jnp.zeros((8, tok), jnp.int32)
+    for block in range(tok // BLK):
+        inside = (token >= block * BLK) & (token < (block + 1) * BLK)
+        kept = jnp.where(inside, flags_ref[block], kept)
+    before = token + first < clip_ref[0]
+    return jnp.where(before & (kept == 1), 1.0, 0.0).astype(f32)[:1]
+
+
 def step_kernel(
     chips, depth, pieces,
     q_hbm, k_hbm, v_hbm, qt_hbm, kt_hbm, vt_hbm, t_hbm, w_hbm, gain_ref, clip_ref, flags_ref,
-    res_ref, gq_ref, gk_ref, gv_ref,
+    res_hbm, gq_hbm, grad_ref,
     q, k, v, qt, kt, vt, teach, weight, loads,
     wide1, near1, sent1, out1, half1, mine1, parts1,
     wide2, near2, sent2, out2, half2, mine2, parts2,
-    unnorm, scale, normed, ngrad, ugrad, turned, gain,
+    unnorm, scale, normed, ngrad, ugrad, turned, gain, res_ref, gq_ref, stores,
     *sems,
 ):
     at = Where(chips, depth)
@@ -196,14 +206,8 @@
     for load in incoming:
         load.start()
 
-    token = lax.broadcasted_iota(jnp.int32, (8, tok), 1)
     device = lax.axis_index("seq") * depth + at.sub
-    kept = jnp.zeros((8, tok), jnp.int32)
-    for block in range(tok // BLK):
-        inside = (token >= block * BLK) & (token < (block + 1) * BLK)
-        kept = jnp.where(inside, flags_ref[block], kept)
-    before = token + device * tok < clip_ref[0]
-    valid = jnp.where(before & (kept == 1), 1.0, 0.0).astype(f32)[:1]
+    valid = kept_tokens(tok, device * tok, clip_ref, flags_ref)
 
     def head(ref, h):
         return ref[h * E : (h + 1) * E, :]
@@ -265,6 +269,9 @@
 
     velocity = dot(turned[...], normed[...], (1, 0))
     res_ref[...] = (velocity - teach[...].astype(f32)).astype(bf16)
+    res_out = pltpu.make_async_copy(res_ref, res_hbm, stores.at[0])
+    gq_out = pltpu.make_async_copy(gq_ref, gq_hbm, stores.at[1])
+    res_out.start()
     ngrad[...] = dot(weight[...], res_ref[...], (1, 0))
     for h in range(H):
         rows = slice(h * E, (h + 1) * E)
@@ -277,17 +284,48 @@
         for h in range(H):
             back = dot(square(wide1, h)[:E], head(ugrad, h), (0, 0))
             gq_ref[h * E : (h + 1) * E, :] = (query(h)[1] * back).astype(bf16)
+        gq_out.start()
 
     all_total(
         at, pieces[1], wide2, near2, sent2, out2, half2, mine2, parts2, sems[8:], None, query_grads
     )
 
+    grad_ref[...] = wide2[...].astype(bf16)
+    res_out.wait()
+    gq_out.wait()
+
+
+def finish_kernel(
+    first_ref, k_hbm, v_hbm, res_hbm, gq_hbm, grad_ref, clip_ref, flags_ref,
+    res_out, gq_out, gk_out, gv_out,
+    k, v, res, gq, gk, gv, loads, stores,
+):
+    tok = k.shape[1]
+    pairs = [(k_hbm, k), (v_hbm, v), (res_hbm, res), (gq_hbm, gq)]
+    incoming = [pltpu.make_async_copy(*pair, loads.at[i]) for i, pair in enumerate(pairs)]
+    pairs = [(res, res_out), (gq, gq_out), (gk, gk_out), (gv, gv_out)]
+    outgoing = [pltpu.make_async_copy(*pair, stores.at[i]) for i, pair in enumerate(pairs)]
+    for load in incoming:
+        load.start()
+    valid = kept_tokens(tok, first_ref[0], clip_ref, flags_ref)
+    incoming[0].wait()
+    incoming[1].wait()
     for h in range(H):
-        total = square(wide2, h)
-        feat, slope = key_parts(h)
         rows = slice(h * E, (h + 1) * E)
-        gk_ref[rows, :] = (slope * dot(total, head(v, h), (0, 0))).astype(bf16)
-        gv_ref[rows, :] = dot(total, feat.astype(bf16), (1, 0)).astype(bf16)
+        total = grad_ref[:, rows]
+        keys = k[rows, :].astype(f32)
+        slope = jnp.where(keys > 0, 1.0, 0.0) * valid
+        feat = (jnp.maximum(keys, 0.0) * valid).astype(bf16)
+        gk[rows, :] = (slope * dot(total, v[rows, :], (0, 0))).astype(bf16)
+        gv[rows, :] = dot(total, feat, (1, 0)).astype(bf16)
+        if h == 1:
+            for load, store in zip(incoming[2:], outgoing[:2]):
+                load.wait()
+                store.start()
+    outgoing[2].start()
+    outgoing[3].start()
+    for store in outgoing:
+        store.wait()
 
 
 def local(
@@ -323,16 +361,13 @@
     anywhere = pl.BlockSpec(memory_space=pl.ANY)
     in_vmem = pl.BlockSpec(memory_space=vmem)
     in_smem = pl.BlockSpec(memory_space=pltpu.SMEM)
-    outs = pl.pallas_call(
+    wide_t = jax.ShapeDtypeStruct((width, tok), bf16)
+    res_t = jax.ShapeDtypeStruct(teacher.shape[::-1], bf16)
+    res, grad_query, grad = pl.pallas_call(
         functools.partial(step_kernel, chips, depth, pieces),
-        out_shape=(
-            jax.ShapeDtypeStruct(teacher.shape[::-1], bf16),
-            jax.ShapeDtypeStruct((width, tok), bf16),
-            jax.ShapeDtypeStruct((width, tok), bf16),
-            jax.ShapeDtypeStruct((width, tok), bf16),
-        ),
+        out_shape=(res_t, wide_t, jax.ShapeDtypeStruct((E, padded), bf16)),
         in_specs=[anywhere] * 8 + [in_vmem, in_smem, in_smem],
-        out_specs=[in_vmem] * 4,
+        out_specs=[anywhere, anywhere, in_vmem],
         scratch_shapes=[vmem(array.shape, array.dtype) for array in arrays]
         + [dma((8,))]
         + totals
@@ -344,10 +379,24 @@
             vmem((width, tok), bf16),
             vmem(out_weight.shape[::-1], bf16),
             vmem((width, 1), f32),
+            vmem(res_t.shape, bf16),
+            vmem((width, tok), bf16),
+            dma((2,)),
         ]
         + ([dma, dma] + [dma((chips,))] * 6) * 2,
         compiler_params=pltpu.CompilerParams(collective_id=0, has_side_effects=True),
     )(*arrays, norm_gain[None, :], clip_length, block_mask)
+    first = (lax.axis_index("seq") * depth + lax.axis_index("sub")) * tok
+    outs = pl.pallas_call(
+        finish_kernel,
+        out_shape=(res_t, wide_t, wide_t, wide_t),
+        in_specs=[in_smem] + [anywhere] * 4 + [in_vmem, in_smem, in_smem],
+        out_specs=[anywhere] * 4,
+        scratch_shapes=[vmem(wide_t.shape, bf16)] * 2
+        + [vmem(res_t.shape, bf16)]
+        + [vmem(wide_t.shape, bf16)] * 3
+        + [dma((4,)), dma((4,))],
+    )(first[None], arrays[1], arrays[2], res, grad_query, grad, clip_length, block_mask)
     return tuple(out.T for out in outs)
 
 

time: 55.5 us -> 53.7 us (0.968)
  local copies, waits for them, and re-layouts: 6.58 us -> 1.29 us
  Pallas kernels: 47.4 us -> 50.9 us
    unnamed x10 -> x0, local copies, waits for them, and re-layouts: 5.28 us -> none
    pallas_call x0 -> x1, Pallas kernels: none -> 4.28 us  [local(): pl.pallas_call(finish_kernel, out_shape=(res_t, wide_t, wide_t, wide_t),...]
    pallas_call x1, Pallas kernels: 47.4 us -> 46.6 us  [local(): pl.pallas_call(functools.partial(step_kernel, chips, depth, pieces), out_...]
where the time goes in v4:
time: 53.7 us; the launch traced here: 53.4 us
  Pallas kernels  50.9 us (95%)
  local copies, waits for them, and re-layouts  1.29 us (2%)
  between operations  1.29 us (2%)
    pallas_call x1, Pallas kernels, local(): pl.pallas_call(functools.partial(step_kernel, chips, depth, pieces), out_...  46.6 us
    pallas_call x1, Pallas kernels, local(): pl.pallas_call(finish_kernel, out_shape=(res_t, wide_t, wide_t, wide_t),...  4.28 us
    broadcast_in_dim x1, local copies, waits for them, and re-layouts, local(): norm_gain[None, :]  1.29 us

profile of v4, /device:TPU:0, one launch (start us, length us, event | category | flops | bytes accessed | tf_op | source)
XLA Modules:
  0.0 53.4 jit_solution(9841083479865095243)
XLA Ops:
  1.3 1.3 %broadcast_in_dim.7.gain_ref = f32[1,1120]{1,0:T(1,128)} reshape(f32[1120]{0:T(1024)} %param.19) | data formatting | bytes 8960 | tf_op jit(solution)/shard_map/broadcast_in_dim | solution.py:388
  2.6 46.6 %shard_map.138 = (bf16[2240,256]{1,0:T(8,128)(2,1)}, bf16[1120,256]{1,0:T(8,128)(2,1)}, bf16[112,1152]{1,0:T(8,128)(2,1)}) custom-call(bf16[1120,256]{1,0:T(8,128)(2,1)} %bitcast.17, bf16[1120,256]{1,0:T(8,128)(2,1)} %bitcast.12, bf16[1120,256]{1,0:T(8,128)(2,1)} %bitcast.14, bf16[1120,256]{1,0:T(8,128)(2,1)} %bitcast.18, bf16[1120,256]{1,0:T(8,128)(2,1)} %bitcast.19, ...), custom_call_target="tpu_custom_call" | custom-call | tf_op jit(solution)/shard_map/pallas_call | solution.py:366
  49.2 4.3 %shard_map.139 = (bf16[2240,256]{1,0:T(8,128)(2,1)}, bf16[1120,256]{1,0:T(8,128)(2,1)}, bf16[1120,256]{1,0:T(8,128)(2,1)}, bf16[1120,256]{1,0:T(8,128)(2,1)}) custom-call(s32[1]{0:T(128)} %bitcast.first_ref, bf16[1120,256]{1,0:T(8,128)(2,1)} %bitcast.13, bf16[1120,256]{1,0:T(8,128)(2,1)} %bitcast.15, bf16[2240,256]{1,0:T(8,128)(2,1)} %get-tuple-element.11.res_hbm, ...), custom_call_target="tpu_custom_call" | custom-call | tf_op jit(solution)/shard_map/pallas_call | solution.py:390

commit v5 on v4

--- a/solution.py
+++ b/solution.py
@@ -34,7 +34,9 @@
         self.depth = depth
         self.chips = chips
         self.core = lax.rem(seq, 2)
-        self.chip = (seq // 2) * depth + self.sub
+        self.plane = seq // 2
+        self.planes = chips // depth
+        self.chip = self.plane * depth + self.sub
         self.partner = (seq + 1 - 2 * self.core, self.sub)
 
     def peer(self, index):
@@ -51,15 +53,20 @@
     barrier = pltpu.get_barrier_semaphore()
     pl.semaphore_signal(barrier, inc=1, device_id=at.partner, device_id_type=MESH)
 
-    @pl.loop(1, at.chips)
-    def _(step):
-        pl.semaphore_signal(
-            barrier, inc=1, device_id=at.peer(at.ahead(step)), device_id_type=MESH
-        )
-
-
-def all_total(at, piece, wide, near, sent, out, half, mine, parts, sems, between=None, after=None):
-    s0, r0, s1, r1, s2, r2, s3, r3 = sems
+    @pl.loop(1, at.planes)
+    def _(step):
+        to = at.peer(lax.rem(at.plane + step, at.planes) * at.depth + at.sub)
+        pl.semaphore_signal(barrier, inc=1, device_id=to, device_id_type=MESH)
+
+    @pl.loop(1, at.depth)
+    def _(step):
+        to = at.peer(at.plane * at.depth + lax.rem(at.sub + step, at.depth))
+        pl.semaphore_signal(barrier, inc=1, device_id=to, device_id_type=MESH)
+
+
+def all_total(at, piece, wide, near, sent, out, half, mine, parts, sems, hooks):
+    s0, r0, s1, r1, s2, r2, s3, r3, s4, r4, s5, r5 = sems
+    plane, planes, sub, depth = at.plane, at.planes, at.sub, at.depth
     core, chip, chips = at.core, at.chip, at.chips
 
     def copy(src, dst, send, recv, to):
@@ -76,28 +83,65 @@
         base = index if side is None else side * chips + index
         return pl.ds(pl.multiple_of(base * piece, 16), piece)
 
-    def scatter(index, slot):
+    def spot(side, level):
+        return side * depth + level
+
+    def plane_scatter(side, level, slot):
         return copy(
-            mine.at[rows(index)], parts.at[rows(slot)], s1.at[index], r1.at[slot], at.peer(index)
-        )
-
-    def gather(index, slot):
+            mine.at[rows(spot(side, level))],
+            parts.at[rows(spot(slot, level))],
+            s1.at[spot(side, level)],
+            r1.at[spot(slot, level)],
+            at.peer(spot(side, sub)),
+        )
+
+    def deep_scatter(level, slot):
+        return copy(
+            mine.at[rows(spot(plane, level))],
+            parts.at[rows(spot(plane, slot))],
+            s2.at[level],
+            r2.at[slot],
+            at.peer(spot(plane, level)),
+        )
+
+    def deep_gather(level, slot):
         return copy(
             out.at[rows(chip, core)],
-            out.at[rows(slot, core)],
-            s2.at[index],
-            r2.at[slot],
-            at.peer(index),
+            out.at[rows(spot(plane, slot), core)],
+            s3.at[level],
+            r3.at[slot],
+            at.peer(spot(plane, level)),
+        )
+
+    def plane_gather(side, level, slot):
+        return copy(
+            out.at[rows(spot(plane, level), core)],
+            out.at[rows(spot(slot, level), core)],
+            s4.at[spot(side, level)],
+            r4.at[spot(slot, level)],
+            at.peer(spot(side, sub)),
         )
 
     def forward(index, side):
         return copy(
             out.at[rows(index, core)],
             out.at[rows(index, side)],
-            s3.at[index],
-            r3.at[index],
+            s5.at[index],
+            r5.at[index],
             at.partner,
         )
+
+    def side_of(step):
+        return lax.rem(plane + step, planes)
+
+    def side_from(step):
+        return lax.rem(plane + planes - step, planes)
+
+    def level_of(step):
+        return lax.rem(sub + step, depth)
+
+    def level_from(step):
+        return lax.rem(sub + depth - step, depth)
 
     size = wide.shape[0]
     for block in range(wide.shape[1] // LANES):
@@ -112,46 +156,89 @@
     other = pl.ds(pl.multiple_of((1 - core) * (chips * piece), 16), chips * piece)
     swap = copy(sent.at[other], half, s0, r0, at.partner)
     swap.start()
-    if between is not None:
-        between()
     swap.wait()
 
     def pair(index):
         return near[rows(index, core), :] + half[rows(index), :].astype(f32)
 
-    @pl.loop(1, chips)
-    def _(step):
-        index = at.ahead(step)
-        mine[rows(index), :] = pair(index).astype(bf16)
-        scatter(index, chip).start()
-
-    if after is not None:
-        after()
-
-    def add(step, acc):
-        index = at.behind(step)
-        scatter(index, index).wait_recv()
-        return acc + parts[rows(index), :].astype(f32)
-
-    out[rows(chip, core), :] = lax.fori_loop(1, chips, add, pair(chip)).astype(bf16)
-
-    @pl.loop(1, chips)
-    def _(step):
-        gather(at.ahead(step), chip).start()
-
-    forward(chip, core).start()
-
-    @pl.loop(1, chips)
-    def _(step):
-        index = at.behind(step)
-        gather(index, index).wait_recv()
-        forward(index, core).start()
-
-    @pl.loop(1, chips)
-    def _(step):
-        index = at.ahead(step)
-        scatter(index, chip).wait_send()
-        gather(index, chip).wait_send()
+    @pl.loop(1, depth + 1)
+    def _(step):
+        level = level_of(step)
+
+        @pl.loop(1, planes)
+        def _(turn):
+            side = side_of(turn)
+            mine[rows(spot(side, level)), :] = pair(spot(side, level)).astype(bf16)
+            plane_scatter(side, level, plane).start()
+
+    hooks[0]()
+
+    def plane_sum(level):
+        def add(turn, acc):
+            side = side_from(turn)
+            plane_scatter(side, level, side).wait_recv()
+            return acc + parts[rows(spot(side, level)), :].astype(f32)
+
+        return lax.fori_loop(1, planes, add, pair(spot(plane, level)))
+
+    @pl.loop(1, depth)
+    def _(step):
+        level = level_of(step)
+        mine[rows(spot(plane, level)), :] = plane_sum(level).astype(bf16)
+        deep_scatter(level, sub).start()
+
+    own = plane_sum(sub)
+    hooks[1]()
+
+    def deep_add(step, acc):
+        level = level_from(step)
+        deep_scatter(level, level).wait_recv()
+        return acc + parts[rows(spot(plane, level)), :].astype(f32)
+
+    out[rows(chip, core), :] = lax.fori_loop(1, depth, deep_add, own).astype(bf16)
+
+    @pl.loop(1, depth)
+    def _(step):
+        deep_gather(level_of(step), sub).start()
+
+    def spread(level):
+        @pl.loop(1, planes)
+        def _(turn):
+            plane_gather(side_of(turn), level, plane).start()
+
+        forward(spot(plane, level), core).start()
+
+    spread(sub)
+
+    @pl.loop(1, depth)
+    def _(step):
+        level = level_from(step)
+        deep_gather(level, level).wait_recv()
+        spread(level)
+
+    @pl.loop(0, depth)
+    def _(step):
+        level = level_from(step)
+
+        @pl.loop(1, planes)
+        def _(turn):
+            side = side_from(turn)
+            plane_gather(side, level, side).wait_recv()
+            forward(spot(side, level), core).start()
+
+    @pl.loop(1, depth)
+    def _(step):
+        deep_scatter(level_of(step), sub).wait_send()
+        deep_gather(level_of(step), sub).wait_send()
+
+    @pl.loop(0, depth)
+    def _(step):
+        level = level_from(step)
+
+        @pl.loop(1, planes)
+        def _(turn):
+            plane_scatter(side_of(turn), level, plane).wait_send()
+            plane_gather(side_of(turn), level, plane).wait_send()
 
     @pl.loop(0, chips)
     def _(step):
@@ -242,13 +329,20 @@
             gain[h * E : (h + 1) * E, :] = jnp.sum(spread, axis=1, keepdims=True)
         for load in incoming[4:]:
             load.wait()
-        for start in range(0, weight.shape[1], 256):
+        turn(0, 5)
+
+    def turn(first, last):
+        for block in range(first, last):
+            start = block * 256
             stop = min(start + 256, weight.shape[1])
             turned[start:stop, :] = weight[:, start:stop].T
 
-    pl.semaphore_wait(pltpu.get_barrier_semaphore(), chips)
+    def turn_rest():
+        turn(5, pl.cdiv(weight.shape[1], 256))
+
+    pl.semaphore_wait(pltpu.get_barrier_semaphore(), at.planes + depth - 1)
     all_total(
-        at, pieces[0], wide1, near1, sent1, out1, half1, mine1, parts1, sems[:8], None, prepare
+        at, pieces[0], wide1, near1, sent1, out1, half1, mine1, parts1, sems[:12], (prepare, turn_rest)
     )
 
     def query(h):
@@ -287,7 +381,7 @@
         gq_out.start()
 
     all_total(
-        at, pieces[1], wide2, near2, sent2, out2, half2, mine2, parts2, sems[8:], None, query_grads
+        at, pieces[1], wide2, near2, sent2, out2, half2, mine2, parts2, sems[12:], (lambda: None, query_grads)
     )
 
     grad_ref[...] = wide2[...].astype(bf16)
@@ -383,7 +477,7 @@
             vmem((width, tok), bf16),
             dma((2,)),
         ]
-        + ([dma, dma] + [dma((chips,))] * 6) * 2,
+        + ([dma, dma] + [dma((chips,))] * 10) * 2,
         compiler_params=pltpu.CompilerParams(collective_id=0, has_side_effects=True),
     )(*arrays, norm_gain[None, :], clip_length, block_mask)
     first = (lax.axis_index("seq") * depth + lax.axis_index("sub")) * tok

time: 53.7 us -> 58.5 us (1.089)
  Pallas kernels: 50.9 us -> 55.6 us
    pallas_call x1, Pallas kernels: 46.6 us -> 51.4 us  [local(): pl.pallas_call(functools.partial(step_kernel, chips, depth, pieces), out_...]
where the time goes in v5:
time: 58.5 us; the launch traced here: 58.2 us
  Pallas kernels  55.6 us (95%)
  local copies, waits for them, and re-layouts  1.29 us (2%)
  between operations  1.29 us (2%)
    pallas_call x1, Pallas kernels, local(): pl.pallas_call(functools.partial(step_kernel, chips, depth, pieces), out_...  51.4 us
    pallas_call x1, Pallas kernels, local(): pl.pallas_call(finish_kernel, out_shape=(res_t, wide_t, wide_t, wide_t),...  4.28 us
    broadcast_in_dim x1, local copies, waits for them, and re-layouts, local(): norm_gain[None, :]  1.29 us

profile of v5, /device:TPU:0, one launch (start us, length us, event | category | flops | bytes accessed | tf_op | source)
XLA Modules:
  0.0 58.2 jit_solution(209935427621280160)
XLA Ops:
  1.3 1.3 %broadcast_in_dim.7.gain_ref = f32[1,1120]{1,0:T(1,128)} reshape(f32[1120]{0:T(1024)} %param.19) | data formatting | bytes 8960 | tf_op jit(solution)/shard_map/broadcast_in_dim | solution.py:482
  2.6 51.4 %shard_map.138 = (bf16[2240,256]{1,0:T(8,128)(2,1)}, bf16[1120,256]{1,0:T(8,128)(2,1)}, bf16[112,1152]{1,0:T(8,128)(2,1)}) custom-call(bf16[1120,256]{1,0:T(8,128)(2,1)} %bitcast.17, bf16[1120,256]{1,0:T(8,128)(2,1)} %bitcast.12, bf16[1120,256]{1,0:T(8,128)(2,1)} %bitcast.14, bf16[1120,256]{1,0:T(8,128)(2,1)} %bitcast.18, bf16[1120,256]{1,0:T(8,128)(2,1)} %bitcast.19, ...), custom_call_target="tpu_custom_call" | custom-call | tf_op jit(solution)/shard_map/pallas_call | solution.py:460
  53.9 4.3 %shard_map.139 = (bf16[2240,256]{1,0:T(8,128)(2,1)}, bf16[1120,256]{1,0:T(8,128)(2,1)}, bf16[1120,256]{1,0:T(8,128)(2,1)}, bf16[1120,256]{1,0:T(8,128)(2,1)}) custom-call(s32[1]{0:T(128)} %bitcast.first_ref, bf16[1120,256]{1,0:T(8,128)(2,1)} %bitcast.13, bf16[1120,256]{1,0:T(8,128)(2,1)} %bitcast.15, bf16[2240,256]{1,0:T(8,128)(2,1)} %get-tuple-element.11.res_hbm, ...), custom_call_target="tpu_custom_call" | custom-call | tf_op jit(solution)/shard_map/pallas_call | solution.py:484
